TPU v7x, 32 devices: a whole 2x2x4 slice. The times are simulated.
32 devices in a mesh: sector: 8 (over z, y), mpo: 4 (over x, core).
Axes of the slice: x: 2, y: 2, z: 4, core: 2. Of those that a mesh axis runs over, the one named last changes fastest.
Arguments:
- vectors: bfloat16 [16, 8, 256, 256], P(None, 'sector'), may hold values from -6 to 6
- left_env: bfloat16 [16, 8, 256, 256], P('mpo', 'sector'), may hold values from -4 to 4
- right_env: bfloat16 [16, 8, 256, 256], P('mpo', 'sector'), may hold values from -4 to 4
- bond_shift: int32 [16], replicated, may hold values from -1 to 1, as said below
Outputs:
- sigma: bfloat16 [16, 8, 256, 256], P('mpo', 'sector')
- intersection: float32 [16, 16], replicated
- ham_small: float32 [16, 16], replicated
Inputs may be any that keep to these rules, and one draw needn't show every extreme that they name: `bond_shift`: every one of -1, 0 and 1 occurs.
All inputs are finite; a program needn't handle non-finite values.
Results may differ from a plain program's by a relative error of at most 0.0034.
Values may be sent and summed in bfloat16 or wider, within the bound.
A program may use at most 128 MiB of HBM per device.

v0:
```python
import jax
import jax.numpy as jnp
from jax import lax
from jax.sharding import PartitionSpec as P


def with_halo(cells, sides, width):
    for axis, dim in sides:
        count = lax.axis_size(axis)
        ends = count - 1
        head = lax.slice_in_dim(cells, 0, width, axis=dim)
        tail = lax.slice_in_dim(cells, cells.shape[dim] - width, cells.shape[dim], axis=dim)
        cells = jnp.concatenate(
            [
                lax.ppermute(tail, axis, [(i, (i + 1) % count) for i in range(ends)]),
                cells,
                lax.ppermute(head, axis, [((i + 1) % count, i) for i in range(ends)]),
            ],
            axis=dim,
        )
    return cells


def bond_term(extended, lenv, renv, shift):
    source = lax.dynamic_slice_in_dim(extended, 1 + shift, lenv.shape[0], 1)
    left = jnp.einsum("sab,vsbc->vsac", lenv, source, preferred_element_type=jnp.float32).astype(
        jnp.bfloat16
    )
    return jnp.einsum("vsac,scd->vsad", left, renv, preferred_element_type=jnp.float32)


def body(vectors, left_env, right_env, bond_shift):
    group = lax.axis_size("mpo")
    per_owner = vectors.shape[0] // group
    owner_start = lax.axis_index("mpo") * per_owner
    owned = lax.dynamic_slice_in_dim(vectors, owner_start, per_owner, 0)
    extended = with_halo(owned, (("sector", 1),), 1)
    empty = jnp.zeros(owned.shape, jnp.float32)
    lpiece = lax.all_gather(left_env, "mpo", axis=0, tiled=True)
    rpiece = lax.all_gather(right_env, "mpo", axis=0, tiled=True)

    def step(index, accum):
        shift = lax.dynamic_index_in_dim(bond_shift, index, 0, keepdims=False)
        return accum + bond_term(extended, lpiece[index], rpiece[index], shift)

    summed = lax.fori_loop(0, lpiece.shape[0], step, empty)
    sigma = summed.astype(jnp.bfloat16)
    scale = 1.0 / (lax.axis_size("sector") * vectors.shape[1] * vectors.shape[2] * vectors.shape[3])
    zeros_small = jnp.zeros((vectors.shape[0], vectors.shape[0]), jnp.float32)
    ham_cols = jnp.einsum("isab,jsab->ij", vectors, sigma, preferred_element_type=jnp.float32)
    ham_part = lax.dynamic_update_slice(zeros_small, ham_cols, (jnp.int32(0), owner_start))
    full_intersection = jnp.einsum(
        "isab,jsab->ij", vectors, vectors, preferred_element_type=jnp.float32
    )
    intersection = lax.psum(full_intersection, "sector")
    ham_small = lax.psum(ham_part, ("sector", "mpo"))
    return (sigma, intersection * scale, ham_small * scale)


def solution(mesh):
    return jax.shard_map(
        body,
        mesh=mesh,
        in_specs=(
            P(None, "sector", None, None),
            P("mpo", "sector", None, None),
            P("mpo", "sector", None, None),
            P(),
        ),
        out_specs=(P("mpo", "sector", None, None), P(), P()),
        check_vma=False,
    )
```

profile of v0, /device:TPU:0, one launch (start us, length us, event | category | flops | bytes accessed | tf_op | source)
XLA Modules:
  0.0 170.0 jit_solution(12909830077423487255)
XLA Ops:
  7.2 0.0 all-gather.3.cloned.1.call-start
  7.2 0.7 all-gather.3.cloned.1.call-update
  7.9 0.0 all-gather.5.cloned.1.call-start
  7.9 0.7 all-gather.5.cloned.1.call-update
  8.7 1.1 constant_dynamic-slice_fusion
  9.7 0.2 copy.29
  9.9 4.9 %collective-permute-start = (bf16[4,1,256,256]{2,3,0,1:T(8,128)(2,1)S(1)}, bf16[4,1,256,256]{2,3,0,1:T(8,128)(2,1)S(1)}, u32[]{:S(2)}, u32[]{:S(2)}) collective-permute-start(bf16[4,1,256,256]{2,3,0,1:T(8,128)(2,1)S(1)} %copy.29), channel_id=1, source_target_pairs={{0,4},{4,8},{8,12},{12,16},{16,20},{20,24},{24,28},{1,5},{5,9},{9,... | collective-permute-start | bytes 1572872 | tf_op jit(solution)/shard_map/ppermute | solution.py:15
  14.9 1.3 collective-permute-start.1
  16.2 4.9 %fusion.18 = f32[16,16]{1,0:T(8,128)S(1)} fusion(bf16[16,256,256]{2,1,0:T(8,128)(2,1)} %bitcast.55), kind=kOutput, calls=%fused_computation.16 | convolution fusion | flops 33554432 | bytes 2098176 | tf_op jit(solution)/shard_map/isab,jsab->ij/dot_general | solution.py:52
  21.1 0.0 copy-start.2
  21.1 29.0 %psum.14 = f32[16,16]{1,0:T(8,128)S(1)} all-reduce(f32[16,16]{1,0:T(8,128)S(1)} %fusion.18), channel_id=1, replica_groups=mesh['sector'=8,'mpo'=4] {'sector'}, use_global_device_ids=true, to_apply=%region_2.3 | all-reduce | flops 256 | bytes 2048 | tf_op jit(solution)/shard_map/psum | solution.py:55
  50.0 0.6 broadcast_multiply_fusion.1
  50.6 0.0 collective-permute-done
  50.6 0.0 copy-start.1
  50.6 0.8 copy-done.1
  51.4 0.0 collective-permute-done.1
  51.4 1.4 pad_maximum_fusion
  52.8 0.0 all-gather.3.cloned.1.call-done
  52.8 6.2 %all-gather.5.cloned.1.call-done = bf16[16,1,256,256]{3,2,1,0:T(8,128)(2,1)} async-done(((bf16[4,1,256,256]{3,2,1,0:T(8,128)(2,1)}), bf16[16,1,256,256]{3,2,1,0:T(8,128)(2,1)}) %all-gather.5.cloned.1.call-update) | async-done | bytes 2097168 | tf_op jit(solution)/shard_map/all_gather | solution.py:39
  59.0 0.0 copy-done.2
  59.0 60.5 %while.16 = (s32[]{:T(128)}, f32[4,1,256,256]{2,3,0,1:T(8,128)S(1)}, bf16[16,1,256,256]{3,2,1,0:T(8,128)(2,1)}, s32[16]{0:T(128)S(1)}, bf16[4,3,256,256]{2,3,0,1...) while((s32[]{:T(128)}, ...), condition=%wide.region_1.2_spmd.clone, body=%wide.region_0.1_spmd.clone.sunk | while | flops 269221888 | bytes 2884781 | solution.py:46
  59.0 0.6 dynamic_slice.71
  60.9 1.9 %fusion.32 = f32[4,1,256,256]{2,3,0,1:T(8,128)S(1)} fusion(f32[4,1,256,256]{2,3,0,1:T(8,128)S(1)} %get-tuple-element.245, bf16[4,3,256,256]{2,3,0,1:T(8,128)(2,1)S(1)} %get-tuple-element.258, s32[]{:T(128)S(6)} %select_n.28, pred[]{:T(512)S(6)} %compare.3, bf16[16,1,256,256]{3,2,1,0:T(8,128)(2,1)} %get-tuple-element.259, s32[]{:T(128)} %get-tuple-element.244, ...), kind=kOutput, calls=%fused_computation.1.clone.1 | convolution fusion | flops 269221888 | bytes 2884613 | tf_op jit(solution)/shard_map/while/body/eval_jaxpr/vsac,scd->vsad/dot_general | solution.py:29
  62.8 0.6 dynamic_slice.71
  64.7 1.9 %fusion.32 = f32[4,1,256,256]{2,3,0,1:T(8,128)S(1)} fusion(f32[4,1,256,256]{2,3,0,1:T(8,128)S(1)} %get-tuple-element.245, bf16[4,3,256,256]{2,3,0,1:T(8,128)(2,1)S(1)} %get-tuple-element.258, s32[]{:T(128)S(6)} %select_n.28, pred[]{:T(512)S(6)} %compare.3, bf16[16,1,256,256]{3,2,1,0:T(8,128)(2,1)} %get-tuple-element.259, s32[]{:T(128)} %get-tuple-element.244, ...), kind=kOutput, calls=%fused_computation.1.clone.1 | convolution fusion | flops 269221888 | bytes 2884613 | tf_op jit(solution)/shard_map/while/body/eval_jaxpr/vsac,scd->vsad/dot_general | solution.py:29
  66.6 0.6 dynamic_slice.71
  68.5 1.9 %fusion.32 = f32[4,1,256,256]{2,3,0,1:T(8,128)S(1)} fusion(f32[4,1,256,256]{2,3,0,1:T(8,128)S(1)} %get-tuple-element.245, bf16[4,3,256,256]{2,3,0,1:T(8,128)(2,1)S(1)} %get-tuple-element.258, s32[]{:T(128)S(6)} %select_n.28, pred[]{:T(512)S(6)} %compare.3, bf16[16,1,256,256]{3,2,1,0:T(8,128)(2,1)} %get-tuple-element.259, s32[]{:T(128)} %get-tuple-element.244, ...), kind=kOutput, calls=%fused_computation.1.clone.1 | convolution fusion | flops 269221888 | bytes 2884613 | tf_op jit(solution)/shard_map/while/body/eval_jaxpr/vsac,scd->vsad/dot_general | solution.py:29
  70.3 0.6 dynamic_slice.71
  72.2 1.9 %fusion.32 = f32[4,1,256,256]{2,3,0,1:T(8,128)S(1)} fusion(f32[4,1,256,256]{2,3,0,1:T(8,128)S(1)} %get-tuple-element.245, bf16[4,3,256,256]{2,3,0,1:T(8,128)(2,1)S(1)} %get-tuple-element.258, s32[]{:T(128)S(6)} %select_n.28, pred[]{:T(512)S(6)} %compare.3, bf16[16,1,256,256]{3,2,1,0:T(8,128)(2,1)} %get-tuple-element.259, s32[]{:T(128)} %get-tuple-element.244, ...), kind=kOutput, calls=%fused_computation.1.clone.1 | convolution fusion | flops 269221888 | bytes 2884613 | tf_op jit(solution)/shard_map/while/body/eval_jaxpr/vsac,scd->vsad/dot_general | solution.py:29
  74.1 0.6 dynamic_slice.71
  76.0 1.9 %fusion.32 = f32[4,1,256,256]{2,3,0,1:T(8,128)S(1)} fusion(f32[4,1,256,256]{2,3,0,1:T(8,128)S(1)} %get-tuple-element.245, bf16[4,3,256,256]{2,3,0,1:T(8,128)(2,1)S(1)} %get-tuple-element.258, s32[]{:T(128)S(6)} %select_n.28, pred[]{:T(512)S(6)} %compare.3, bf16[16,1,256,256]{3,2,1,0:T(8,128)(2,1)} %get-tuple-element.259, s32[]{:T(128)} %get-tuple-element.244, ...), kind=kOutput, calls=%fused_computation.1.clone.1 | convolution fusion | flops 269221888 | bytes 2884613 | tf_op jit(solution)/shard_map/while/body/eval_jaxpr/vsac,scd->vsad/dot_general | solution.py:29
  77.9 0.6 dynamic_slice.71
  79.8 1.9 %fusion.32 = f32[4,1,256,256]{2,3,0,1:T(8,128)S(1)} fusion(f32[4,1,256,256]{2,3,0,1:T(8,128)S(1)} %get-tuple-element.245, bf16[4,3,256,256]{2,3,0,1:T(8,128)(2,1)S(1)} %get-tuple-element.258, s32[]{:T(128)S(6)} %select_n.28, pred[]{:T(512)S(6)} %compare.3, bf16[16,1,256,256]{3,2,1,0:T(8,128)(2,1)} %get-tuple-element.259, s32[]{:T(128)} %get-tuple-element.244, ...), kind=kOutput, calls=%fused_computation.1.clone.1 | convolution fusion | flops 269221888 | bytes 2884613 | tf_op jit(solution)/shard_map/while/body/eval_jaxpr/vsac,scd->vsad/dot_general | solution.py:29
  81.7 0.6 dynamic_slice.71
  83.6 1.9 %fusion.32 = f32[4,1,256,256]{2,3,0,1:T(8,128)S(1)} fusion(f32[4,1,256,256]{2,3,0,1:T(8,128)S(1)} %get-tuple-element.245, bf16[4,3,256,256]{2,3,0,1:T(8,128)(2,1)S(1)} %get-tuple-element.258, s32[]{:T(128)S(6)} %select_n.28, pred[]{:T(512)S(6)} %compare.3, bf16[16,1,256,256]{3,2,1,0:T(8,128)(2,1)} %get-tuple-element.259, s32[]{:T(128)} %get-tuple-element.244, ...), kind=kOutput, calls=%fused_computation.1.clone.1 | convolution fusion | flops 269221888 | bytes 2884613 | tf_op jit(solution)/shard_map/while/body/eval_jaxpr/vsac,scd->vsad/dot_general | solution.py:29
  85.5 0.6 dynamic_slice.71
  87.4 1.9 %fusion.32 = f32[4,1,256,256]{2,3,0,1:T(8,128)S(1)} fusion(f32[4,1,256,256]{2,3,0,1:T(8,128)S(1)} %get-tuple-element.245, bf16[4,3,256,256]{2,3,0,1:T(8,128)(2,1)S(1)} %get-tuple-element.258, s32[]{:T(128)S(6)} %select_n.28, pred[]{:T(512)S(6)} %compare.3, bf16[16,1,256,256]{3,2,1,0:T(8,128)(2,1)} %get-tuple-element.259, s32[]{:T(128)} %get-tuple-element.244, ...), kind=kOutput, calls=%fused_computation.1.clone.1 | convolution fusion | flops 269221888 | bytes 2884613 | tf_op jit(solution)/shard_map/while/body/eval_jaxpr/vsac,scd->vsad/dot_general | solution.py:29
  89.2 0.6 dynamic_slice.71
  91.1 1.9 %fusion.32 = f32[4,1,256,256]{2,3,0,1:T(8,128)S(1)} fusion(f32[4,1,256,256]{2,3,0,1:T(8,128)S(1)} %get-tuple-element.245, bf16[4,3,256,256]{2,3,0,1:T(8,128)(2,1)S(1)} %get-tuple-element.258, s32[]{:T(128)S(6)} %select_n.28, pred[]{:T(512)S(6)} %compare.3, bf16[16,1,256,256]{3,2,1,0:T(8,128)(2,1)} %get-tuple-element.259, s32[]{:T(128)} %get-tuple-element.244, ...), kind=kOutput, calls=%fused_computation.1.clone.1 | convolution fusion | flops 269221888 | bytes 2884613 | tf_op jit(solution)/shard_map/while/body/eval_jaxpr/vsac,scd->vsad/dot_general | solution.py:29
  93.0 0.6 dynamic_slice.71
  94.9 1.9 %fusion.32 = f32[4,1,256,256]{2,3,0,1:T(8,128)S(1)} fusion(f32[4,1,256,256]{2,3,0,1:T(8,128)S(1)} %get-tuple-element.245, bf16[4,3,256,256]{2,3,0,1:T(8,128)(2,1)S(1)} %get-tuple-element.258, s32[]{:T(128)S(6)} %select_n.28, pred[]{:T(512)S(6)} %compare.3, bf16[16,1,256,256]{3,2,1,0:T(8,128)(2,1)} %get-tuple-element.259, s32[]{:T(128)} %get-tuple-element.244, ...), kind=kOutput, calls=%fused_computation.1.clone.1 | convolution fusion | flops 269221888 | bytes 2884613 | tf_op jit(solution)/shard_map/while/body/eval_jaxpr/vsac,scd->vsad/dot_general | solution.py:29
  96.8 0.6 dynamic_slice.71
  98.7 1.9 %fusion.32 = f32[4,1,256,256]{2,3,0,1:T(8,128)S(1)} fusion(f32[4,1,256,256]{2,3,0,1:T(8,128)S(1)} %get-tuple-element.245, bf16[4,3,256,256]{2,3,0,1:T(8,128)(2,1)S(1)} %get-tuple-element.258, s32[]{:T(128)S(6)} %select_n.28, pred[]{:T(512)S(6)} %compare.3, bf16[16,1,256,256]{3,2,1,0:T(8,128)(2,1)} %get-tuple-element.259, s32[]{:T(128)} %get-tuple-element.244, ...), kind=kOutput, calls=%fused_computation.1.clone.1 | convolution fusion | flops 269221888 | bytes 2884613 | tf_op jit(solution)/shard_map/while/body/eval_jaxpr/vsac,scd->vsad/dot_general | solution.py:29
  100.6 0.6 dynamic_slice.71
  102.5 1.9 %fusion.32 = f32[4,1,256,256]{2,3,0,1:T(8,128)S(1)} fusion(f32[4,1,256,256]{2,3,0,1:T(8,128)S(1)} %get-tuple-element.245, bf16[4,3,256,256]{2,3,0,1:T(8,128)(2,1)S(1)} %get-tuple-element.258, s32[]{:T(128)S(6)} %select_n.28, pred[]{:T(512)S(6)} %compare.3, bf16[16,1,256,256]{3,2,1,0:T(8,128)(2,1)} %get-tuple-element.259, s32[]{:T(128)} %get-tuple-element.244, ...), kind=kOutput, calls=%fused_computation.1.clone.1 | convolution fusion | flops 269221888 | bytes 2884613 | tf_op jit(solution)/shard_map/while/body/eval_jaxpr/vsac,scd->vsad/dot_general | solution.py:29
  104.4 0.6 dynamic_slice.71
  106.3 1.9 %fusion.32 = f32[4,1,256,256]{2,3,0,1:T(8,128)S(1)} fusion(f32[4,1,256,256]{2,3,0,1:T(8,128)S(1)} %get-tuple-element.245, bf16[4,3,256,256]{2,3,0,1:T(8,128)(2,1)S(1)} %get-tuple-element.258, s32[]{:T(128)S(6)} %select_n.28, pred[]{:T(512)S(6)} %compare.3, bf16[16,1,256,256]{3,2,1,0:T(8,128)(2,1)} %get-tuple-element.259, s32[]{:T(128)} %get-tuple-element.244, ...), kind=kOutput, calls=%fused_computation.1.clone.1 | convolution fusion | flops 269221888 | bytes 2884613 | tf_op jit(solution)/shard_map/while/body/eval_jaxpr/vsac,scd->vsad/dot_general | solution.py:29
  108.1 0.6 dynamic_slice.71
  110.0 1.9 %fusion.32 = f32[4,1,256,256]{2,3,0,1:T(8,128)S(1)} fusion(f32[4,1,256,256]{2,3,0,1:T(8,128)S(1)} %get-tuple-element.245, bf16[4,3,256,256]{2,3,0,1:T(8,128)(2,1)S(1)} %get-tuple-element.258, s32[]{:T(128)S(6)} %select_n.28, pred[]{:T(512)S(6)} %compare.3, bf16[16,1,256,256]{3,2,1,0:T(8,128)(2,1)} %get-tuple-element.259, s32[]{:T(128)} %get-tuple-element.244, ...), kind=kOutput, calls=%fused_computation.1.clone.1 | convolution fusion | flops 269221888 | bytes 2884613 | tf_op jit(solution)/shard_map/while/body/eval_jaxpr/vsac,scd->vsad/dot_general | solution.py:29
  111.9 0.6 dynamic_slice.71
  113.8 1.9 %fusion.32 = f32[4,1,256,256]{2,3,0,1:T(8,128)S(1)} fusion(f32[4,1,256,256]{2,3,0,1:T(8,128)S(1)} %get-tuple-element.245, bf16[4,3,256,256]{2,3,0,1:T(8,128)(2,1)S(1)} %get-tuple-element.258, s32[]{:T(128)S(6)} %select_n.28, pred[]{:T(512)S(6)} %compare.3, bf16[16,1,256,256]{3,2,1,0:T(8,128)(2,1)} %get-tuple-element.259, s32[]{:T(128)} %get-tuple-element.244, ...), kind=kOutput, calls=%fused_computation.1.clone.1 | convolution fusion | flops 269221888 | bytes 2884613 | tf_op jit(solution)/shard_map/while/body/eval_jaxpr/vsac,scd->vsad/dot_general | solution.py:29
  115.7 0.6 dynamic_slice.71
  117.6 1.9 %fusion.32 = f32[4,1,256,256]{2,3,0,1:T(8,128)S(1)} fusion(f32[4,1,256,256]{2,3,0,1:T(8,128)S(1)} %get-tuple-element.245, bf16[4,3,256,256]{2,3,0,1:T(8,128)(2,1)S(1)} %get-tuple-element.258, s32[]{:T(128)S(6)} %select_n.28, pred[]{:T(512)S(6)} %compare.3, bf16[16,1,256,256]{3,2,1,0:T(8,128)(2,1)} %get-tuple-element.259, s32[]{:T(128)} %get-tuple-element.244, ...), kind=kOutput, calls=%fused_computation.1.clone.1 | convolution fusion | flops 269221888 | bytes 2884613 | tf_op jit(solution)/shard_map/while/body/eval_jaxpr/vsac,scd->vsad/dot_general | solution.py:29
  119.5 0.2 copy.19
  119.7 0.0 copy-start
  119.7 3.3 %fusion.21 = f32[16,4]{1,0:T(8,128)S(1)} fusion(bf16[16,256,256]{2,1,0:T(8,128)(2,1)} %bitcast.56, bf16[4,256,256]{2,1,0:T(8,128)(2,1)S(1)} %bitcast.54), kind=kOutput, calls=%fused_computation.17 | convolution fusion | flops 8388608 | bytes 2621696 | tf_op jit(solution)/shard_map/isab,jsab->ij/dot_general | solution.py:50
  122.9 0.0 copy-done
  123.0 0.2 dynamic_update_slice.3
  123.2 39.4 %psum.15 = f32[16,16]{1,0:T(8,128)S(1)} all-reduce(f32[16,16]{1,0:T(8,128)S(1)} %dynamic_update_slice.3), channel_id=1, replica_groups=mesh['sector'=8,'mpo'=4] {'sector','mpo'}, use_global_device_ids=true, to_apply=%region_3.4 | all-reduce | flops 256 | bytes 2048 | tf_op jit(solution)/shard_map/psum | solution.py:56
  162.6 0.6 broadcast_multiply_fusion
  (2 shorter events, 0.0 us)
Async XLA Ops:
  7.2 45.7 %all-gather.3.cloned.1.call-start = ((), (), s32[]{:S(2)}) async-start(), calls=%async_computation | async-start | bytes 2621440 | tf_op jit(solution)/shard_map/all_gather | solution.py:40
  7.9 51.1 %all-gather.5.cloned.1.call-start = ((), (), s32[]{:S(2)}) async-start(), calls=%async_computation.1 | async-start | bytes 2621440 | tf_op jit(solution)/shard_map/all_gather | solution.py:39
  9.9 40.7 %collective-permute-start = (bf16[4,1,256,256]{2,3,0,1:T(8,128)(2,1)S(1)}, bf16[4,1,256,256]{2,3,0,1:T(8,128)(2,1)S(1)}, u32[]{:S(2)}, u32[]{:S(2)}) collective-permute-start(bf16[4,1,256,256]{2,3,0,1:T(8,128)(2,1)S(1)} %copy.29), channel_id=1, source_target_pairs={{0,4},{4,8},{8,12},{12,16},{16,20},{20,24},{24,28},{1,5},{5,9},{9,... | collective-permute-start | bytes 1572872 | tf_op jit(solution)/shard_map/ppermute | solution.py:15
  14.9 36.5 %collective-permute-start.1 = (bf16[4,1,256,256]{2,3,0,1:T(8,128)(2,1)S(1)}, bf16[4,1,256,256]{2,3,0,1:T(8,128)(2,1)}, u32[]{:S(2)}, u32[]{:S(2)}) collective-permute-start(bf16[4,1,256,256]{2,3,0,1:T(8,128)(2,1)S(1)} %copy.29), channel_id=1, source_target_pairs={{4,0},{8,4},{12,8},{16,12},{20,16},{24,20},{28,24},{5,1},{9,5},{13... | collective-permute-start | bytes 1572872 | tf_op jit(solution)/shard_map/ppermute | solution.py:17
  21.1 38.0 %copy-start.2 = (s32[16]{0:T(128)S(1)}, s32[16]{0:T(128)}, u32[]{:S(2)}) copy-start(s32[16]{0:T(128)} %param.9) | copy-start | bytes 196
  50.6 0.8 copy-start.1
  119.7 3.3 %copy-start = (bf16[4,1,256,256]{3,2,1,0:T(8,128)(2,1)}, bf16[4,1,256,256]{3,2,1,0:T(8,128)(2,1)S(1)}, u32[]{:S(2)}) copy-start(bf16[4,1,256,256]{3,2,1,0:T(8,128)(2,1)S(1)} %copy.19) | copy-start | bytes 1572868
Sparse Core Ops, SparseCore 0:
  9.5 25.2 all-gather.2
  36.4 22.5 all-gather.4
where the time goes:
time: 171 us; the launch traced here: 170 us
  blocking collectives  68.3 us (40%)
  matrix products  38 us (22%)
  loops' own time  21.2 us (12%)
  between operations  14.1 us (8%)
  local copies, waits for them, and re-layouts  11.9 us (7%)
  waiting for transfers between devices  7.58 us (4%)
  starting transfers between devices  6.3 us (4%)
  other arithmetic  2.58 us (2%)
    psum x1, blocking collectives, body(): ham_small = lax.psum(ham_part, ('sector', 'mpo'))  39.4 us
    dot_general x16, matrix products, bond_term(): jnp.einsum('vsac,scd->vsad', left, renv, preferred_element_type=jnp.float32)  29.9 us
    psum x1, blocking collectives, body(): intersection = lax.psum(full_intersection, 'sector')  29 us
    another operation x1, loops' own time, body(): summed = lax.fori_loop(0, lpiece.shape[0], step, empty)  21.2 us
    dynamic_slice x16, local copies, waits for them, and re-layouts, step(): shift = lax.dynamic_index_in_dim(bond_shift, index, 0, keepdims=False)  9.38 us
    all_gather x1, waiting for transfers between devices, body(): lpiece = lax.all_gather(left_env, 'mpo', axis=0, tiled=True)  6.17 us
    ppermute x1, starting transfers between devices, with_halo(): lax.ppermute(tail, axis, [(i, (i + 1) % count) for i in range(ends)])  4.93 us
    dot_general x1, matrix products, body(): jnp.einsum('isab,jsab->ij', vectors, vectors, preferred_element_type=jnp....  4.86 us
  transfers between devices with their start and end apart: 4, of which 1 were waited for; matrix products, arithmetic and copies ran while one was open for 5% of the time, Pallas kernels for 0%

commit v1 on v0

v1 whole, which is shorter than its diff:
```python
import functools

import jax
import jax.numpy as jnp
from jax import lax
from jax.experimental import pallas as pl
from jax.experimental.pallas import tpu as pltpu
from jax.sharding import PartitionSpec as P

MESH = pl.DeviceIdType.MESH
F32 = jnp.float32
BF16 = jnp.bfloat16


def dot(a, b):
    return jnp.dot(a, b, preferred_element_type=F32)


def gram_row(vall, cols, first, nv, per):
    rows = vall.shape[1]
    blk = vall.shape[2]
    prod = jnp.zeros((per * nv, nv * nv), F32)
    for r in range(rows // nv):
        x = vall[:, r * nv : (r + 1) * nv, :].reshape(nv * nv, blk)
        y = cols[:, r * nv : (r + 1) * nv, :].reshape(per * nv, blk)
        prod += lax.dot_general(y, x, (((1,), (1,)), ((), ())), preferred_element_type=F32)
    sub = lax.broadcasted_iota(jnp.int32, prod.shape, 0) % nv
    lane = lax.broadcasted_iota(jnp.int32, prod.shape, 1) % nv
    prod = jnp.where(sub == lane, prod, 0.0)
    summed = jnp.concatenate(
        [jnp.sum(prod[j * nv : (j + 1) * nv], axis=0, keepdims=True) for j in range(per)], axis=0
    )
    width = nv * nv
    place = lax.broadcasted_iota(jnp.int32, summed.shape, 1) % nv
    step = 1
    while step < nv:
        up = pltpu.roll(summed, step, 1)
        down = pltpu.roll(summed, width - step, 1)
        summed = summed + jnp.where((place // step) % 2 == 1, up, down)
        step *= 2
    which = lax.broadcasted_iota(jnp.int32, summed.shape, 0)
    return jnp.sum(jnp.where(place == first + which, summed, 0.0), axis=0, keepdims=True)


def kernel(n_sec, n_mpo, nv, per, nb, scale, vec, left, right, shift, sigma, inter, ham, *scratch):
    ext = scratch[:per]
    (
        env_l, env_r, vall, acc, row_i, row_h, all_i, all_h,
        loc_sem, pair_s, pair_r, fwd_s, fwd_r, x_s, x_r, die_s, die_r,
        small_s, small_r,
    ) = scratch[per:]
    chips = n_mpo // 2
    total = n_sec * n_mpo
    sec = lax.axis_index("sector")
    mpo = lax.axis_index("mpo")
    me = sec * n_mpo + mpo
    core = mpo % 2
    chip = mpo // 2
    partner = chip * 2 + (1 - core)

    barrier = pltpu.get_barrier_semaphore()

    def greet(k, carry):
        other = (me + k) % total
        pl.semaphore_signal(
            barrier, inc=1, device_id=(other // n_mpo, other % n_mpo), device_id_type=MESH
        )
        return carry

    lax.fori_loop(1, total, greet, 0)
    pl.semaphore_wait(barrier, total - 1)

    par = sec % 2
    pair = sec + 1 - 2 * par
    slot_pair = 2 - 2 * par
    slot_fwd = 2 * par
    ahead = sec + 2 * (1 - 2 * par)
    behind = sec - 2 * (1 - 2 * par)
    has_ahead = (ahead >= 0) & (ahead < n_sec)
    has_behind = (behind >= 0) & (behind < n_sec)

    def remote(src, dst, send, recv, target):
        return pltpu.make_async_remote_copy(
            src_ref=src, dst_ref=dst, send_sem=send, recv_sem=recv,
            device_id=target, device_id_type=MESH,
        )

    def x_copies(d, k):
        target = (sec, ((chip + d) % chips) * 2 + core)
        slot = 2 * d
        return (
            remote(left.at[k, 0], env_l.at[slot, k], x_s.at[d, 0, k], x_r.at[d, 0, k], target),
            remote(right.at[k, 0], env_r.at[slot, k], x_s.at[d, 1, k], x_r.at[d, 1, k], target),
        )

    def die_copies(d, k):
        target = (sec, partner)
        src_l = left.at[k, 0] if d == 0 else env_l.at[2 * d, k]
        src_r = right.at[k, 0] if d == 0 else env_r.at[2 * d, k]
        return (
            remote(src_l, env_l.at[2 * d + 1, k], die_s.at[d, 0, k], die_r.at[d, 0, k], target),
            remote(src_r, env_r.at[2 * d + 1, k], die_s.at[d, 1, k], die_r.at[d, 1, k], target),
        )

    def pair_copy(v):
        return remote(
            vec.at[mpo * per + v, 0], ext[v].at[slot_fwd], pair_s.at[v], pair_r.at[v], (pair, mpo)
        )

    def fwd_copy(v):
        return remote(
            ext[v].at[slot_pair], ext[v].at[slot_fwd], fwd_s.at[v], fwd_r.at[v], (ahead, mpo)
        )

    for k in range(nb):
        for d in range(1, chips):
            for c in x_copies(d, k):
                c.start()
        if k < per:
            pair_copy(k).start()
    for v in range(nb, per):
        pair_copy(v).start()
    local = [
        pltpu.make_async_copy(left.at[:, 0], env_l.at[0], loc_sem.at[0]),
        pltpu.make_async_copy(right.at[:, 0], env_r.at[0], loc_sem.at[1]),
        pltpu.make_async_copy(vec.at[:, 0], vall, loc_sem.at[2]),
    ] + [
        pltpu.make_async_copy(vec.at[mpo * per + v, 0], ext[v].at[1], loc_sem.at[3 + v])
        for v in range(per)
    ]
    for c in local:
        c.start()
    for k in range(nb):
        for c in die_copies(0, k):
            c.start()

    @pl.when(jnp.logical_not(has_behind))
    def _():
        for v in range(per):
            ext[v][slot_fwd] = jnp.zeros(ext[v].shape[1:], BF16)

    acc[...] = jnp.zeros_like(acc)
    for c in local:
        c.wait()

    def share(row, rows, which):
        rows[me] = row[...]

        def send(k, carry):
            other = (me + k) % total
            remote(
                row, rows.at[me], small_s.at[which], small_r.at[which],
                (other // n_mpo, other % n_mpo),
            ).start()
            return carry

        lax.fori_loop(1, total, send, 0)

    def collect(rows, out, which):
        most = rows.at[pl.ds(0, total - 1)]
        pltpu.make_async_copy(most, most, small_s.at[which]).wait()
        pltpu.make_async_copy(most, most, small_r.at[which]).wait()

        def add(k, carry):
            return carry + rows[k]

        line = lax.fori_loop(0, total, add, jnp.zeros(rows.shape[1:], F32)) * scale
        for i in range(nv):
            out[i : i + 1, :] = line[:, i * nv : (i + 1) * nv]

    def forward(v):
        pair_copy(v).wait_recv()

        @pl.when(has_ahead)
        def _():
            fwd_copy(v).start()

    def bond(slot, k):
        d = slot // 2
        from_chip = (chip + chips - d) % chips
        from_core = (core + slot % 2) % 2
        return (from_chip * 2 + from_core) * nb + k

    def near_terms(v):
        @pl.when(has_behind)
        def _():
            fwd_copy(v).wait_recv()

        def step(it, carry):
            slot = it // nb
            k = it % nb
            src = ext[v][1 + shift[bond(slot, k)]]
            mid = dot(env_l[slot, k], src).astype(BF16)
            acc[v] += dot(mid, env_r[slot, k])
            return carry

        lax.fori_loop(0, 2 * nb, step, 0)

    def far_term(slot, k):
        sh = 1 + shift[bond(slot, k)]
        lhs = env_l[slot, k]
        rhs = env_r[slot, k]
        for v in range(per):
            acc[v] += dot(dot(lhs, ext[v][sh]).astype(BF16), rhs)

    forward(0)
    own = jnp.stack([ext[v][1] for v in range(per)], axis=0)
    row_i[...] = gram_row(vall, own, mpo * per, nv, per)
    share(row_i, all_i, 0)
    for k in range(nb):
        for c in die_copies(0, k):
            c.wait_recv()
    for v in range(per):
        if v + 1 < per:
            forward(v + 1)
        near_terms(v)

    for d in range(1, chips):

        def arrive(k, carry):
            for c in x_copies(d, k):
                c.wait_recv()
            for c in die_copies(d, k):
                c.start()
            far_term(2 * d, k)
            for c in die_copies(d, k):
                c.wait_recv()
            far_term(2 * d + 1, k)
            return carry

        lax.fori_loop(0, nb, arrive, 0)

    sigma[:, 0] = acc[...].astype(BF16)
    row_h[...] = gram_row(vall, sigma[:, 0], mpo * per, nv, per)
    share(row_h, all_h, 1)
    collect(all_i, inter, 0)

    for k in range(nb):
        for d in range(chips):
            for c in die_copies(d, k):
                c.wait_send()
            if d:
                for c in x_copies(d, k):
                    c.wait_send()
    for v in range(per):
        pair_copy(v).wait_send()

    @pl.when(has_ahead)
    def _():
        for v in range(per):
            fwd_copy(v).wait_send()

    collect(all_h, ham, 1)


def body(vectors, left_env, right_env, bond_shift):
    n_sec = lax.axis_size("sector")
    n_mpo = lax.axis_size("mpo")
    nv, _, rows, blk = vectors.shape
    nb = left_env.shape[0]
    per = nv // n_mpo
    total = n_sec * n_mpo
    chips = n_mpo // 2
    scale = 1.0 / (n_sec * vectors.shape[1] * rows * blk)
    any_spec = pl.BlockSpec(memory_space=pl.ANY)
    vmem_spec = pl.BlockSpec(memory_space=pltpu.VMEM)
    dma = pltpu.SemaphoreType.DMA
    return pl.pallas_call(
        functools.partial(kernel, n_sec, n_mpo, nv, per, nb, scale),
        out_shape=(
            jax.ShapeDtypeStruct((per, 1, rows, blk), BF16),
            jax.ShapeDtypeStruct((nv, nv), F32),
            jax.ShapeDtypeStruct((nv, nv), F32),
        ),
        in_specs=[any_spec] * 3 + [pl.BlockSpec(memory_space=pltpu.SMEM)],
        out_specs=(vmem_spec,) * 3,
        scratch_shapes=[pltpu.VMEM((3, rows, blk), BF16) for _ in range(per)]
        + [
            pltpu.VMEM((n_mpo, nb, rows, rows), BF16),
            pltpu.VMEM((n_mpo, nb, blk, blk), BF16),
            pltpu.VMEM((nv, rows, blk), BF16),
            pltpu.VMEM((per, rows, blk), F32),
            pltpu.VMEM((1, nv * nv), F32),
            pltpu.VMEM((1, nv * nv), F32),
            pltpu.VMEM((total, 1, nv * nv), F32),
            pltpu.VMEM((total, 1, nv * nv), F32),
            dma((3 + per,)),
            dma((per,)), dma((per,)), dma((per,)), dma((per,)),
            dma((chips, 2, nb)), dma((chips, 2, nb)),
            dma((chips, 2, nb)), dma((chips, 2, nb)),
            dma((2,)), dma((2,)),
        ],
        compiler_params=pltpu.CompilerParams(
            collective_id=0, has_side_effects=True, vmem_limit_bytes=48 << 20
        ),
        name="davidson",
    )(vectors, left_env, right_env, bond_shift)


def solution(mesh):
    return jax.shard_map(
        body,
        mesh=mesh,
        in_specs=(
            P(None, "sector", None, None),
            P("mpo", "sector", None, None),
            P("mpo", "sector", None, None),
            P(),
        ),
        out_specs=(P("mpo", "sector", None, None), P(), P()),
        check_vma=False,
    )
```

time: 171 us -> 49.8 us (0.29)
  blocking collectives: 68.3 us -> 0 us
  Pallas kernels: 0 us -> 42.6 us
  matrix products: 38 us -> 0 us
  loops' own time: 21.2 us -> 0 us
  between operations: 14.1 us -> 0.65 us
  waiting for transfers between devices: 7.58 us -> 0 us
  starting transfers between devices: 6.3 us -> 0 us
  local copies, waits for them, and re-layouts: 11.9 us -> 6.31 us
  other arithmetic: 2.58 us -> 0 us
    psum x2 -> x0, blocking collectives: 68.3 us -> none  [the longest x1 39.4 us: body(): ham_small = lax.psum(ham_part, ('sector', 'mpo'))]
    pallas_call x0 -> x1, Pallas kernels: none -> 42.6 us  [body(): pl.pallas_call(functools.partial(kernel, n_sec, n_mpo, nv, per, nb, scale...]
    dot_general x18 -> x0, matrix products: 38 us -> none  [the longest x16 29.9 us: bond_term(): jnp.einsum('vsac,scd->vsad', left, renv, preferred_element_type=jnp.float32)]
    another operation x1 -> x0, loops' own time: 21.2 us -> none  [body(): summed = lax.fori_loop(0, lpiece.shape[0], step, empty)]
    dynamic_slice x17 -> x0, local copies, waits for them, and re-layouts: 10.5 us -> none  [the longest x16 9.38 us: step(): shift = lax.dynamic_index_in_dim(bond_shift, index, 0, keepdims=False)]
    ppermute x2 -> x0, starting transfers between devices: 6.22 us -> none  [the longest x1 4.93 us: with_halo(): lax.ppermute(tail, axis, [(i, (i + 1) % count) for i in range(ends)])]
    all_gather x2 -> x0, waiting for transfers between devices: 6.19 us -> none  [the longest x1 6.17 us: body(): lpiece = lax.all_gather(left_env, 'mpo', axis=0, tiled=True)]
    unnamed x7 -> x11, local copies, waits for them, and re-layouts: 1.01 us -> 6.31 us
  transfers between devices with their start and end apart: 4 -> 0, of which waited for: 1 -> 0; matrix products, arithmetic and copies ran while one was open for 5% -> 0% of each run, Pallas kernels for 0% -> 0%
where the time goes in v1:
time: 49.8 us; the launch traced here: 49.5 us
  Pallas kernels  42.6 us (86%)
  local copies, waits for them, and re-layouts  6.31 us (13%)
  between operations  0.65 us (1%)
    pallas_call x1, Pallas kernels, body(): pl.pallas_call(functools.partial(kernel, n_sec, n_mpo, nv, per, nb, scale...  42.6 us
    unnamed x11, local copies, waits for them, and re-layouts  6.31 us

profile of v1, /device:TPU:0, one launch (start us, length us, event | category | flops | bytes accessed | tf_op | source)
XLA Modules:
  0.0 49.5 jit_solution(9965518885636237959)
XLA Ops:
  0.6 0.0 copy-start
  0.6 1.6 %copy-done = bf16[16,1,256,256]{3,2,1,0:T(8,128)(2,1)S(1)} copy-done((bf16[16,1,256,256]{3,2,1,0:T(8,128)(2,1)S(1)}, bf16[16,1,256,256]{3,2,1,0:T(8,128)(2,1)}, u32[]{:S(2)}) %copy-start) | copy-done | bytes 2097176
  2.2 0.0 copy-start.1
  2.2 1.0 %copy-done.1 = bf16[4,1,256,256]{3,2,1,0:T(8,128)(2,1)S(1)} copy-done((bf16[4,1,256,256]{3,2,1,0:T(8,128)(2,1)S(1)}, bf16[4,1,256,256]{3,2,1,0:T(8,128)(2,1)}, u32[]{:S(2)}) %copy-start.1) | copy-done | bytes 524312
  3.3 0.0 copy-start.2
  3.3 1.0 %copy-done.2 = bf16[4,1,256,256]{3,2,1,0:T(8,128)(2,1)S(1)} copy-done((bf16[4,1,256,256]{3,2,1,0:T(8,128)(2,1)S(1)}, bf16[4,1,256,256]{3,2,1,0:T(8,128)(2,1)}, u32[]{:S(2)}) %copy-start.2) | copy-done | bytes 524312
  4.3 0.0 copy-start.3
  4.3 0.7 %copy-done.3 = s32[16]{0:T(128)S(1)} copy-done((s32[16]{0:T(128)S(1)}, s32[16]{0:T(128)}, u32[]{:S(2)}) %copy-start.3) | copy-done | bytes 88
  5.0 42.6 %davidson.1 = (bf16[4,1,256,256]{3,2,1,0:T(8,128)(2,1)S(1)}, f32[16,16]{1,0:T(8,128)S(1)}, f32[16,16]{1,0:T(8,128)S(1)}) custom-call(bf16[16,1,256,256]{3,2,1,0:T(8,128)(2,1)S(1)} %copy-done, bf16[4,1,256,256]{3,2,1,0:T(8,128)(2,1)S(1)} %copy-done.1, bf16[4,1,256,256]{3,2,1,0:T(8,128)(2,1)S(1)} %copy-done.2, s32[16]{0:T(128)S(1)} %copy-done.3), custom_call_target="tpu_custom_call" | custom-call | tf_op jit(solution)/shard_map/davidson/pallas_call | solution.py:268
  47.5 0.8 %copy.10 = bf16[4,1,256,256]{3,2,1,0:T(8,128)(2,1)} copy(bf16[4,1,256,256]{3,2,1,0:T(8,128)(2,1)S(1)} %get-tuple-element.6) | data formatting | bytes 1048576
  48.3 0.6 %copy.11 = f32[16,16]{1,0:T(8,128)} copy(f32[16,16]{1,0:T(8,128)S(1)} %get-tuple-element.7) | data formatting | bytes 2048
  48.9 0.6 %copy.12 = f32[16,16]{1,0:T(8,128)} copy(f32[16,16]{1,0:T(8,128)S(1)} %get-tuple-element.8) | data formatting | bytes 2048
Async XLA Ops:
  0.6 1.6 %copy-start = (bf16[16,1,256,256]{3,2,1,0:T(8,128)(2,1)S(1)}, bf16[16,1,256,256]{3,2,1,0:T(8,128)(2,1)}, u32[]{:S(2)}) copy-start(bf16[16,1,256,256]{3,2,1,0:T(8,128)(2,1)} %vec.1) | copy-start | bytes 6291460
  2.2 1.0 %copy-start.1 = (bf16[4,1,256,256]{3,2,1,0:T(8,128)(2,1)S(1)}, bf16[4,1,256,256]{3,2,1,0:T(8,128)(2,1)}, u32[]{:S(2)}) copy-start(bf16[4,1,256,256]{3,2,1,0:T(8,128)(2,1)} %left.1) | copy-start | bytes 1572868
  3.3 1.0 %copy-start.2 = (bf16[4,1,256,256]{3,2,1,0:T(8,128)(2,1)S(1)}, bf16[4,1,256,256]{3,2,1,0:T(8,128)(2,1)}, u32[]{:S(2)}) copy-start(bf16[4,1,256,256]{3,2,1,0:T(8,128)(2,1)} %right.1) | copy-start | bytes 1572868
  4.3 0.7 %copy-start.3 = (s32[16]{0:T(128)S(1)}, s32[16]{0:T(128)}, u32[]{:S(2)}) copy-start(s32[16]{0:T(128)} %shift.1) | copy-start | bytes 196

commit v2 on v1

--- a/solution.py
+++ b/solution.py
@@ -47,7 +47,7 @@
     (
         env_l, env_r, vall, acc, row_i, row_h, all_i, all_h,
         loc_sem, pair_s, pair_r, fwd_s, fwd_r, x_s, x_r, die_s, die_r,
-        small_s, small_r,
+        small_s, small_r, token,
     ) = scratch[per:]
     chips = n_mpo // 2
     total = n_sec * n_mpo
@@ -58,18 +58,6 @@
     chip = mpo // 2
     partner = chip * 2 + (1 - core)
 
-    barrier = pltpu.get_barrier_semaphore()
-
-    def greet(k, carry):
-        other = (me + k) % total
-        pl.semaphore_signal(
-            barrier, inc=1, device_id=(other // n_mpo, other % n_mpo), device_id_type=MESH
-        )
-        return carry
-
-    lax.fori_loop(1, total, greet, 0)
-    pl.semaphore_wait(barrier, total - 1)
-
     par = sec % 2
     pair = sec + 1 - 2 * par
     slot_pair = 2 - 2 * par
@@ -79,6 +67,42 @@
     has_ahead = (ahead >= 0) & (ahead < n_sec)
     has_behind = (behind >= 0) & (behind < n_sec)
 
+    barrier = pltpu.get_barrier_semaphore()
+
+    def greet(target):
+        pl.semaphore_signal(barrier, inc=1, device_id=target, device_id_type=MESH)
+
+    for d in range(1, n_mpo):
+        greet((sec, (mpo + d) % n_mpo))
+    for d in range(n_mpo):
+        greet((pair, (mpo + d) % n_mpo))
+
+    @pl.when(has_ahead)
+    def _():
+        greet((ahead, mpo))
+
+    @pl.when(has_behind)
+    def _():
+        greet((behind, mpo))
+
+    pl.semaphore_wait(
+        barrier, 2 * n_mpo - 1 + has_ahead.astype(jnp.int32) + has_behind.astype(jnp.int32)
+    )
+
+    def pass_tokens():
+        @pl.when(has_behind)
+        def _():
+            pl.semaphore_wait(token.at[0], 1)
+
+        @pl.when(has_ahead)
+        def _():
+            pl.semaphore_signal(token.at[0], inc=1, device_id=(ahead, mpo), device_id_type=MESH)
+            pl.semaphore_wait(token.at[1], 1)
+
+        @pl.when(has_behind)
+        def _():
+            pl.semaphore_signal(token.at[1], inc=1, device_id=(behind, mpo), device_id_type=MESH)
+
     def remote(src, dst, send, recv, target):
         return pltpu.make_async_remote_copy(
             src_ref=src, dst_ref=dst, send_sem=send, recv_sem=recv,
@@ -87,19 +111,18 @@
 
     def x_copies(d, k):
         target = (sec, ((chip + d) % chips) * 2 + core)
-        slot = 2 * d
         return (
-            remote(left.at[k, 0], env_l.at[slot, k], x_s.at[d, 0, k], x_r.at[d, 0, k], target),
-            remote(right.at[k, 0], env_r.at[slot, k], x_s.at[d, 1, k], x_r.at[d, 1, k], target),
+            remote(left.at[k, 0], env_l.at[d, k, 0], x_s.at[d, 0, k], x_r.at[d, 0, k], target),
+            remote(right.at[k, 0], env_r.at[d, k, 0], x_s.at[d, 1, k], x_r.at[d, 1, k], target),
         )
 
     def die_copies(d, k):
         target = (sec, partner)
-        src_l = left.at[k, 0] if d == 0 else env_l.at[2 * d, k]
-        src_r = right.at[k, 0] if d == 0 else env_r.at[2 * d, k]
+        src_l = left.at[k, 0] if d == 0 else env_l.at[d, k, 0]
+        src_r = right.at[k, 0] if d == 0 else env_r.at[d, k, 0]
         return (
-            remote(src_l, env_l.at[2 * d + 1, k], die_s.at[d, 0, k], die_r.at[d, 0, k], target),
-            remote(src_r, env_r.at[2 * d + 1, k], die_s.at[d, 1, k], die_r.at[d, 1, k], target),
+            remote(src_l, env_l.at[d, k, 1], die_s.at[d, 0, k], die_r.at[d, 0, k], target),
+            remote(src_r, env_r.at[d, k, 1], die_s.at[d, 1, k], die_r.at[d, 1, k], target),
         )
 
     def pair_copy(v):
@@ -121,8 +144,8 @@
     for v in range(nb, per):
         pair_copy(v).start()
     local = [
-        pltpu.make_async_copy(left.at[:, 0], env_l.at[0], loc_sem.at[0]),
-        pltpu.make_async_copy(right.at[:, 0], env_r.at[0], loc_sem.at[1]),
+        pltpu.make_async_copy(left.at[:, 0], env_l.at[0, :, 0], loc_sem.at[0]),
+        pltpu.make_async_copy(right.at[:, 0], env_r.at[0, :, 0], loc_sem.at[1]),
         pltpu.make_async_copy(vec.at[:, 0], vall, loc_sem.at[2]),
     ] + [
         pltpu.make_async_copy(vec.at[mpo * per + v, 0], ext[v].at[1], loc_sem.at[3 + v])
@@ -139,6 +162,7 @@
         for v in range(per):
             ext[v][slot_fwd] = jnp.zeros(ext[v].shape[1:], BF16)
 
+    pass_tokens()
     acc[...] = jnp.zeros_like(acc)
     for c in local:
         c.wait()
@@ -175,11 +199,18 @@
         def _():
             fwd_copy(v).start()
 
-    def bond(slot, k):
-        d = slot // 2
+    def halo(d, k, c):
         from_chip = (chip + chips - d) % chips
-        from_core = (core + slot % 2) % 2
-        return (from_chip * 2 + from_core) * nb + k
+        return 1 + shift[(from_chip * 2 + (core + c) % 2) * nb + k]
+
+    def mid(v, d, k, c):
+        return dot(env_l[d, k, c], ext[v][halo(d, k, c)]).astype(BF16)
+
+    def rights(d, k, count):
+        block = env_r[d, pl.ds(k, count)]
+        return block.reshape(count * 2 * block.shape[2], block.shape[3])
+
+    group = 2 if nb % 2 == 0 else 1
 
     def near_terms(v):
         @pl.when(has_behind)
@@ -187,21 +218,30 @@
             fwd_copy(v).wait_recv()
 
         def step(it, carry):
-            slot = it // nb
-            k = it % nb
-            src = ext[v][1 + shift[bond(slot, k)]]
-            mid = dot(env_l[slot, k], src).astype(BF16)
-            acc[v] += dot(mid, env_r[slot, k])
+            mids = [mid(v, 0, it * group + g, c) for g in range(group) for c in range(2)]
+            acc[v] += dot(jnp.concatenate(mids, axis=1), rights(0, it * group, group))
             return carry
 
-        lax.fori_loop(0, 2 * nb, step, 0)
-
-    def far_term(slot, k):
-        sh = 1 + shift[bond(slot, k)]
-        lhs = env_l[slot, k]
-        rhs = env_r[slot, k]
+        lax.fori_loop(0, nb // group, step, 0)
+
+    def far_terms(d, k, last):
+        cx = x_copies(d, k)
+        cd = die_copies(d, k)
+        cx[0].wait_recv()
+        cd[0].start()
+        first = [mid(v, d, k, 0) for v in range(per)]
+        cx[1].wait_recv()
+        cd[1].start()
+        cd[0].wait_recv()
+        second = [mid(v, d, k, 1) for v in range(per)]
+        cd[1].wait_recv()
+        both = rights(d, k, 1)
         for v in range(per):
-            acc[v] += dot(dot(lhs, ext[v][sh]).astype(BF16), rhs)
+            out = acc[v] + dot(jnp.concatenate([first[v], second[v]], axis=1), both)
+            if last:
+                sigma[v, 0] = out.astype(BF16)
+            else:
+                acc[v] = out
 
     forward(0)
     own = jnp.stack([ext[v][1] for v in range(per)], axis=0)
@@ -218,19 +258,11 @@
     for d in range(1, chips):
 
         def arrive(k, carry):
-            for c in x_copies(d, k):
-                c.wait_recv()
-            for c in die_copies(d, k):
-                c.start()
-            far_term(2 * d, k)
-            for c in die_copies(d, k):
-                c.wait_recv()
-            far_term(2 * d + 1, k)
+            far_terms(d, k, False)
             return carry
 
-        lax.fori_loop(0, nb, arrive, 0)
-
-    sigma[:, 0] = acc[...].astype(BF16)
+        lax.fori_loop(0, nb - (d == chips - 1), arrive, 0)
+    far_terms(chips - 1, nb - 1, True)
     row_h[...] = gram_row(vall, sigma[:, 0], mpo * per, nv, per)
     share(row_h, all_h, 1)
     collect(all_i, inter, 0)
@@ -262,7 +294,7 @@
     total = n_sec * n_mpo
     chips = n_mpo // 2
     scale = 1.0 / (n_sec * vectors.shape[1] * rows * blk)
-    any_spec = pl.BlockSpec(memory_space=pl.ANY)
+    any_spec = pl.BlockSpec(memory_space=pltpu.HBM)
     vmem_spec = pl.BlockSpec(memory_space=pltpu.VMEM)
     dma = pltpu.SemaphoreType.DMA
     return pl.pallas_call(
@@ -276,8 +308,8 @@
         out_specs=(vmem_spec,) * 3,
         scratch_shapes=[pltpu.VMEM((3, rows, blk), BF16) for _ in range(per)]
         + [
-            pltpu.VMEM((n_mpo, nb, rows, rows), BF16),
-            pltpu.VMEM((n_mpo, nb, blk, blk), BF16),
+            pltpu.VMEM((chips, nb, 2, rows, rows), BF16),
+            pltpu.VMEM((chips, nb, 2, blk, blk), BF16),
             pltpu.VMEM((nv, rows, blk), BF16),
             pltpu.VMEM((per, rows, blk), F32),
             pltpu.VMEM((1, nv * nv), F32),
@@ -289,9 +321,10 @@
             dma((chips, 2, nb)), dma((chips, 2, nb)),
             dma((chips, 2, nb)), dma((chips, 2, nb)),
             dma((2,)), dma((2,)),
+            pltpu.SemaphoreType.REGULAR((2,)),
         ],
         compiler_params=pltpu.CompilerParams(
-            collective_id=0, has_side_effects=True, vmem_limit_bytes=48 << 20
+            collective_id=0, has_side_effects=True, vmem_limit_bytes=67043328 - (700 << 10)
         ),
         name="davidson",
     )(vectors, left_env, right_env, bond_shift)

time: 49.8 us -> 45.8 us (0.920)
  Pallas kernels: 42.6 us -> 40.4 us
  local copies, waits for them, and re-layouts: 6.31 us -> 4.46 us
    pallas_call x1, Pallas kernels: 42.6 us -> 40.4 us  [body(): pl.pallas_call(functools.partial(kernel, n_sec, n_mpo, nv, per, nb, scale...]
    unnamed x11 -> x3, local copies, waits for them, and re-layouts: 6.31 us -> 4.46 us
where the time goes in v2:
time: 45.8 us; the launch traced here: 45.5 us
  Pallas kernels  40.4 us (88%)
  local copies, waits for them, and re-layouts  4.46 us (10%)
  between operations  0.64 us (1%)
    pallas_call x1, Pallas kernels, body(): pl.pallas_call(functools.partial(kernel, n_sec, n_mpo, nv, per, nb, scale...  40.4 us
    unnamed x3, local copies, waits for them, and re-layouts  4.46 us

profile of v2, /device:TPU:0, one launch (start us, length us, event | category | flops | bytes accessed | tf_op | source)
XLA Modules:
  0.0 45.5 jit_solution(6527562824087232130)
XLA Ops:
  0.6 40.4 %davidson.1 = (bf16[4,1,256,256]{3,2,1,0:T(8,128)(2,1)}, f32[16,16]{1,0:T(8,128)}, f32[16,16]{1,0:T(8,128)}) custom-call(bf16[16,1,256,256]{3,2,1,0:T(8,128)(2,1)} %vec.1, bf16[4,1,256,256]{3,2,1,0:T(8,128)(2,1)} %left.1, bf16[4,1,256,256]{3,2,1,0:T(8,128)(2,1)} %right.1, s32[16]{0:T(128)} %shift.1), custom_call_target="tpu_custom_call" | custom-call | tf_op jit(solution)/shard_map/davidson/pallas_call | solution.py:300
  41.0 1.9 %copy.10 = bf16[4,1,256,256]{3,2,1,0:T(8,128)(2,1)} copy(bf16[4,1,256,256]{3,2,1,0:T(8,128)(2,1)} %get-tuple-element.6) | data formatting | bytes 1048576
  42.9 1.3 %copy.11 = f32[16,16]{1,0:T(8,128)} copy(f32[16,16]{1,0:T(8,128)} %get-tuple-element.7) | data formatting | bytes 2048
  44.2 1.3 %copy.12 = f32[16,16]{1,0:T(8,128)} copy(f32[16,16]{1,0:T(8,128)} %get-tuple-element.8) | data formatting | bytes 2048

commit v3 on v2

--- a/solution.py
+++ b/solution.py
@@ -324,10 +324,10 @@
             pltpu.SemaphoreType.REGULAR((2,)),
         ],
         compiler_params=pltpu.CompilerParams(
-            collective_id=0, has_side_effects=True, vmem_limit_bytes=67043328 - (700 << 10)
+            collective_id=0, has_side_effects=True, vmem_limit_bytes=52 << 20
         ),
         name="davidson",
-    )(vectors, left_env, right_env, bond_shift)
+    )(*(pltpu.with_memory_space_constraint(x, pltpu.HBM) for x in (vectors, left_env, right_env)), pltpu.with_memory_space_constraint(bond_shift, pltpu.HBM))
 
 
 def solution(mesh):

time: 45.8 us -> 42.5 us (0.928)
  local copies, waits for them, and re-layouts: 4.46 us -> 1.99 us
  Pallas kernels: 40.4 us -> 39.7 us
    unnamed x3, local copies, waits for them, and re-layouts: 4.46 us -> 1.99 us
    pallas_call x1, Pallas kernels: 40.4 us -> 39.7 us  [body(): pl.pallas_call(functools.partial(kernel, n_sec, n_mpo, nv, per, nb, scale...]
where the time goes in v3:
time: 42.5 us; the launch traced here: 42.3 us
  Pallas kernels  39.7 us (93%)
  local copies, waits for them, and re-layouts  1.99 us (5%)
  between operations  0.64 us (2%)
    pallas_call x1, Pallas kernels, body(): pl.pallas_call(functools.partial(kernel, n_sec, n_mpo, nv, per, nb, scale...  39.7 us
    unnamed x3, local copies, waits for them, and re-layouts  1.99 us

profile of v3, /device:TPU:0, one launch (start us, length us, event | category | flops | bytes accessed | tf_op | source)
XLA Modules:
  0.0 42.3 jit_solution(16952974966956177998)
XLA Ops:
  0.6 39.7 %davidson.1 = (bf16[4,1,256,256]{3,2,1,0:T(8,128)(2,1)S(1)}, f32[16,16]{1,0:T(8,128)S(1)}, f32[16,16]{1,0:T(8,128)S(1)}) custom-call(bf16[16,1,256,256]{3,2,1,0:T(8,128)(2,1)} %vec.1, bf16[4,1,256,256]{3,2,1,0:T(8,128)(2,1)} %left.1, bf16[4,1,256,256]{3,2,1,0:T(8,128)(2,1)} %right.1, s32[16]{0:T(128)} %shift.1), custom_call_target="tpu_custom_call" | custom-call | tf_op jit(solution)/shard_map/davidson/pallas_call | solution.py:300
  40.3 0.8 %copy.10 = bf16[4,1,256,256]{3,2,1,0:T(8,128)(2,1)} copy(bf16[4,1,256,256]{3,2,1,0:T(8,128)(2,1)S(1)} %get-tuple-element.6) | data formatting | bytes 1048576
  41.1 0.6 %copy.11 = f32[16,16]{1,0:T(8,128)} copy(f32[16,16]{1,0:T(8,128)S(1)} %get-tuple-element.7) | data formatting | bytes 2048
  41.7 0.6 %copy.12 = f32[16,16]{1,0:T(8,128)} copy(f32[16,16]{1,0:T(8,128)S(1)} %get-tuple-element.8) | data formatting | bytes 2048

commit v4 on v3

--- a/solution.py
+++ b/solution.py
@@ -16,14 +16,12 @@
     return jnp.dot(a, b, preferred_element_type=F32)
 
 
-def gram_row(vall, cols, first, nv, per):
-    rows = vall.shape[1]
-    blk = vall.shape[2]
+def gram_row(turned, cols, first, nv, per):
+    blk = cols.shape[2]
     prod = jnp.zeros((per * nv, nv * nv), F32)
-    for r in range(rows // nv):
-        x = vall[:, r * nv : (r + 1) * nv, :].reshape(nv * nv, blk)
+    for r in range(turned.shape[0]):
         y = cols[:, r * nv : (r + 1) * nv, :].reshape(per * nv, blk)
-        prod += lax.dot_general(y, x, (((1,), (1,)), ((), ())), preferred_element_type=F32)
+        prod += dot(y, turned[r])
     sub = lax.broadcasted_iota(jnp.int32, prod.shape, 0) % nv
     lane = lax.broadcasted_iota(jnp.int32, prod.shape, 1) % nv
     prod = jnp.where(sub == lane, prod, 0.0)
@@ -45,7 +43,7 @@
 def kernel(n_sec, n_mpo, nv, per, nb, scale, vec, left, right, shift, sigma, inter, ham, *scratch):
     ext = scratch[:per]
     (
-        env_l, env_r, vall, acc, row_i, row_h, all_i, all_h,
+        env_l, env_r, vall, turned, acc, row_i, row_h, all_i, all_h,
         loc_sem, pair_s, pair_r, fwd_s, fwd_r, x_s, x_r, die_s, die_r,
         small_s, small_r, token,
     ) = scratch[per:]
@@ -170,25 +168,28 @@
     def share(row, rows, which):
         rows[me] = row[...]
 
-        def send(k, carry):
-            other = (me + k) % total
-            remote(
-                row, rows.at[me], small_s.at[which], small_r.at[which],
-                (other // n_mpo, other % n_mpo),
-            ).start()
+        def send(target):
+            remote(row, rows.at[me], small_s.at[which], small_r.at[which], target).start()
+
+        def sector(k, carry):
+            low = sec < n_sec // 2
+            other = jnp.where(low, n_sec - 1 - k, k)
+            other = jnp.where(low & (other <= sec), other - 1, other)
+            other = jnp.where(jnp.logical_not(low) & (other >= sec), other + 1, other)
+            for m in range(n_mpo):
+                send((other, m))
             return carry
 
-        lax.fori_loop(1, total, send, 0)
+        lax.fori_loop(0, n_sec - 1, sector, 0)
+        for d in range(1, n_mpo):
+            send((sec, (mpo + d) % n_mpo))
 
     def collect(rows, out, which):
         most = rows.at[pl.ds(0, total - 1)]
         pltpu.make_async_copy(most, most, small_s.at[which]).wait()
         pltpu.make_async_copy(most, most, small_r.at[which]).wait()
 
-        def add(k, carry):
-            return carry + rows[k]
-
-        line = lax.fori_loop(0, total, add, jnp.zeros(rows.shape[1:], F32)) * scale
+        line = jnp.sum(rows[...], axis=0) * scale
         for i in range(nv):
             out[i : i + 1, :] = line[:, i * nv : (i + 1) * nv]
 
@@ -245,7 +246,13 @@
 
     forward(0)
     own = jnp.stack([ext[v][1] for v in range(per)], axis=0)
-    row_i[...] = gram_row(vall, own, mpo * per, nv, per)
+    def turn(r, carry):
+        x = vall[:, pl.ds(pl.multiple_of(r * nv, nv), nv), :]
+        turned[r] = x.reshape(nv * nv, x.shape[2]).T
+        return carry
+
+    lax.fori_loop(0, turned.shape[0], turn, 0)
+    row_i[...] = gram_row(turned, own, mpo * per, nv, per)
     share(row_i, all_i, 0)
     for k in range(nb):
         for c in die_copies(0, k):
@@ -263,7 +270,7 @@
 
         lax.fori_loop(0, nb - (d == chips - 1), arrive, 0)
     far_terms(chips - 1, nb - 1, True)
-    row_h[...] = gram_row(vall, sigma[:, 0], mpo * per, nv, per)
+    row_h[...] = gram_row(turned, sigma[:, 0], mpo * per, nv, per)
     share(row_h, all_h, 1)
     collect(all_i, inter, 0)
 
@@ -311,6 +318,7 @@
             pltpu.VMEM((chips, nb, 2, rows, rows), BF16),
             pltpu.VMEM((chips, nb, 2, blk, blk), BF16),
             pltpu.VMEM((nv, rows, blk), BF16),
+            pltpu.VMEM((rows // nv, blk, nv * nv), BF16),
             pltpu.VMEM((per, rows, blk), F32),
             pltpu.VMEM((1, nv * nv), F32),
             pltpu.VMEM((1, nv * nv), F32),

time: 42.5 us -> 41.9 us (0.986)
  Pallas kernels: 39.7 us -> 39.1 us
    pallas_call x1, Pallas kernels: 39.7 us -> 39.1 us  [body(): pl.pallas_call(functools.partial(kernel, n_sec, n_mpo, nv, per, nb, scale...]
where the time goes in v4:
time: 41.9 us; the launch traced here: 41.7 us
  Pallas kernels  39.1 us (93%)
  local copies, waits for them, and re-layouts  1.99 us (5%)
  between operations  0.64 us (2%)
    pallas_call x1, Pallas kernels, body(): pl.pallas_call(functools.partial(kernel, n_sec, n_mpo, nv, per, nb, scale...  39.1 us
    unnamed x3, local copies, waits for them, and re-layouts  1.99 us

profile of v4, /device:TPU:0, one launch (start us, length us, event | category | flops | bytes accessed | tf_op | source)
XLA Modules:
  0.0 41.7 jit_solution(15704369382141884260)
XLA Ops:
  0.6 39.1 %davidson.1 = (bf16[4,1,256,256]{3,2,1,0:T(8,128)(2,1)S(1)}, f32[16,16]{1,0:T(8,128)S(1)}, f32[16,16]{1,0:T(8,128)S(1)}) custom-call(bf16[16,1,256,256]{3,2,1,0:T(8,128)(2,1)} %vec.1, bf16[4,1,256,256]{3,2,1,0:T(8,128)(2,1)} %left.1, bf16[4,1,256,256]{3,2,1,0:T(8,128)(2,1)} %right.1, s32[16]{0:T(128)} %shift.1), custom_call_target="tpu_custom_call" | custom-call | tf_op jit(solution)/shard_map/davidson/pallas_call | solution.py:307
  39.7 0.8 %copy.10 = bf16[4,1,256,256]{3,2,1,0:T(8,128)(2,1)} copy(bf16[4,1,256,256]{3,2,1,0:T(8,128)(2,1)S(1)} %get-tuple-element.6) | data formatting | bytes 1048576
  40.5 0.6 %copy.11 = f32[16,16]{1,0:T(8,128)} copy(f32[16,16]{1,0:T(8,128)S(1)} %get-tuple-element.7) | data formatting | bytes 2048
  41.1 0.6 %copy.12 = f32[16,16]{1,0:T(8,128)} copy(f32[16,16]{1,0:T(8,128)S(1)} %get-tuple-element.8) | data formatting | bytes 2048
